TPU v7x, 32 devices: a whole 2x2x4 slice. The times are simulated.
32 devices in a mesh: ctx: 8 (over y, x, core), ch: 4 (over z).
Axes of the slice: x: 2, y: 2, z: 4, core: 2. Of those that a mesh axis runs over, the one named last changes fastest.
Arguments:
- query_act: bfloat16 [4096, 4096], P('ctx', 'ch'), may hold values from -6 to 6
- key_act: bfloat16 [4096, 4096], P('ctx', 'ch'), may hold values from -6 to 6
- value_act: bfloat16 [4096, 4096], P('ctx', 'ch'), may hold values from -6 to 6
- filters: bfloat16 [4096, 128], P('ch'), may hold values from -0.5 to 0.5
- proj_weight: bfloat16 [8192, 4096], P('ctx', 'ch'), may hold values from -0.09375 to 0.09375
- cotangent: bfloat16 [4096, 8192], P('ctx', 'ch'), may hold values from -6 to 6
Outputs:
- grad_query: bfloat16 [4096, 4096], P('ctx', 'ch')
- grad_key: bfloat16 [4096, 4096], P('ctx', 'ch')
- grad_value: bfloat16 [4096, 4096], P('ctx', 'ch')
- grad_filter: float32 [4096, 128], P('ch')
- grad_proj: float32 [8192, 4096], P('ctx', 'ch')
All inputs are finite; a program needn't handle non-finite values.
Results may differ from a plain program's by a relative error of at most 0.0051.
Values may be sent and summed in bfloat16 or wider, within the bound.
A program may use at most 192 MiB of HBM per device.

v0:
```python
import jax
import jax.numpy as jnp
import numpy as np
from jax import lax
from jax.sharding import PartitionSpec as P

TAPS = 128


def from_behind(x, axis, by):
    length = lax.axis_size(axis)
    pairs = [(i, i + by) for i in range(length) if 0 <= i + by < length]
    return lax.ppermute(x, axis, pairs)


def basis(points):
    freqs = points // 2
    phase = (2 * np.arange(freqs)[:, None] + 1) * np.arange(points)[None, :] % (2 * points)
    angle = np.pi * phase / points
    return np.concatenate([np.cos(angle), np.sin(angle)], 0).astype(np.float32)


def split(a):
    a = jnp.asarray(a, jnp.float32)
    hi = a.astype(jnp.bfloat16)
    return (hi, (a - hi.astype(jnp.float32)).astype(jnp.bfloat16))


def dot32(a, b):
    return jnp.dot(a, b, preferred_element_type=jnp.float32)


def forward(table, x):
    hi, lo = split(table)
    return dot32(hi, x) + dot32(lo, x)


def backward(table, y):
    thi, tlo = split(table)
    yhi, ylo = split(y)
    return dot32(thi, yhi) + dot32(thi, ylo) + dot32(tlo, yhi)


def halves(x):
    n = x.shape[0] // 2
    return (x[:n], x[n:])


def times(x, f):
    (xc, xs), (fc, fs) = (halves(x), halves(f))
    return jnp.concatenate([xc * fc - xs * fs, xc * fs + xs * fc], 0)


def times_conj(x, f):
    (xc, xs), (fc, fs) = (halves(x), halves(f))
    return jnp.concatenate([xc * fc + xs * fs, xs * fc - xc * fs], 0)


def shards(query_act, key_act, value_act, filters, proj_weight, cotangent):
    tokens = query_act.shape[0]
    points = tokens + TAPS
    table = basis(points)
    inverse = (table.T / (points // 2)).astype(np.float32)
    gathered = lax.all_gather(cotangent, "ch", axis=1, tiled=True)
    weight = lax.all_gather(proj_weight, "ctx", axis=0, tiled=True)
    query_f = query_act.astype(jnp.float32)
    key_f = key_act.astype(jnp.float32)
    value_f = value_act.astype(jnp.float32)
    product = (key_f * value_f).astype(jnp.bfloat16)
    before = from_behind(product[tokens - TAPS :], "ctx", 1)
    filt_spec = forward(table[:, :TAPS], filters.T)
    prod_spec = forward(table[:, :TAPS], before) + forward(table[:, TAPS:], product)
    mixed = backward(inverse[TAPS:], times(prod_spec, filt_spec))
    gated = (query_f * mixed).astype(jnp.bfloat16)
    partial_grad = lax.dot_general(
        gathered, gated, (((0,), (0,)), ((), ())), preferred_element_type=jnp.float32
    ).astype(jnp.bfloat16)
    grad_proj = lax.psum_scatter(partial_grad, "ctx", scatter_dimension=0, tiled=True).astype(
        jnp.float32
    )
    grad_mix = dot32(gathered, weight)
    grad_query = (grad_mix * mixed).astype(jnp.bfloat16)
    grad_gate = (grad_mix * query_f).astype(jnp.bfloat16)
    after = from_behind(grad_gate[:TAPS], "ctx", -1)
    own_spec = forward(table[:, :tokens], grad_gate)
    gate_spec = own_spec + forward(table[:, tokens:], after)
    lags = inverse[TAPS - np.arange(TAPS)]
    local_filter = backward(lags, times_conj(prod_spec, own_spec))
    grad_filter = lax.psum(local_filter, "ctx").T
    grad_prod = backward(inverse[:tokens], times_conj(gate_spec, filt_spec))
    grad_key = (grad_prod * value_f).astype(jnp.bfloat16)
    grad_value = (grad_prod * key_f).astype(jnp.bfloat16)
    return (grad_query, grad_key, grad_value, grad_filter, grad_proj)


def solution(mesh):
    return jax.shard_map(
        shards,
        mesh=mesh,
        in_specs=(
            P("ctx", "ch"),
            P("ctx", "ch"),
            P("ctx", "ch"),
            P("ch", None),
            P("ctx", "ch"),
            P("ctx", "ch"),
        ),
        out_specs=(P("ctx", "ch"), P("ctx", "ch"), P("ctx", "ch"), P("ch", None), P("ctx", "ch")),
        check_vma=False,
    )
```

profile of v0, /device:TPU:0, one launch (start us, length us, event | category | flops | bytes accessed | tf_op | source)
XLA Modules:
  0.0 497.0 jit_solution(8108205557831197759)
XLA Ops:
  7.2 0.7 all-gather.3.cloned.1.call-update
  8.0 0.7 all-gather.5.cloned.1.call-update
  8.8 1.3 copy.19
  10.1 1.3 copy.20
  11.4 0.5 fusion.39
  11.9 0.5 convolution_add_fusion
  12.4 149.5 %all-gather.3.cloned.1.call-done = bf16[512,8192]{1,0:T(8,128)(2,1)} async-done(((bf16[512,2048]{1,0:T(8,128)(2,1)}), bf16[512,8192]{1,0:T(8,128)(2,1)}) %all-gather.3.cloned.1.call-update) | async-done | bytes 8388624 | tf_op jit(solution)/shard_map/all_gather | solution.py:64
  162.0 90.0 %all-gather.5.cloned.1.call-done = bf16[8192,1024]{1,0:T(8,128)(2,1)} async-done(((bf16[1024,1024]{1,0:T(8,128)(2,1)}), bf16[8192,1024]{1,0:T(8,128)(2,1)}) %all-gather.5.cloned.1.call-update) | async-done | bytes 16777232 | tf_op jit(solution)/shard_map/all_gather | solution.py:65
  251.9 14.9 %fusion.6 = (bf16[512,1024]{1,0:T(8,128)(2,1)S(1)}, f32[512,1024]{1,0:T(8,128)S(1)}) fusion(bf16[512,1024]{1,0:T(8,128)(2,1)} %param.14, bf16[512,8192]{1,0:T(8,128)(2,1)} %all-gather.3.cloned.1.call-done, bf16[8192,1024]{1,0:T(8,128)(2,1)} %all-gather.5.cloned.1.call-done), kind=kOutput, calls=%fused_computation.20 | convolution fusion | flops 8591507456 | bytes 29360128 | tf_op jit(solution)/shard_map/dot_general | solution.py:30
  266.9 1.4 collective-permute-start.1
  268.4 0.9 fusion.40
  269.2 0.9 convolution_add_fusion.1
  270.1 0.4 collective-permute-done.1
  270.5 0.5 fusion.41
  271.0 0.5 add_add_fusion
  271.5 0.6 multiply_add_fusion.1
  272.2 0.5 copy-done.8
  272.6 1.0 fusion.8
  273.7 1.0 fusion.21
  274.7 0.2 copy-done.5
  274.9 0.3 copy-done.6
  275.2 0.2 copy-done.12
  275.4 2.7 fusion.3
  278.1 6.7 %collective-permute-start = (bf16[128,1024]{0,1:T(8,128)(2,1)S(1)}, bf16[128,1024]{0,1:T(8,128)(2,1)S(1)}, u32[]{:S(2)}, u32[]{:S(2)}) collective-permute-start(bf16[128,1024]{0,1:T(8,128)(2,1)S(1)} %slice.44), channel_id=1, source_target_pairs={{0,4},{4,8},{8,12},{12,16},{16,20},{20,24},{24,28},{1,5},{5,9},{9,... | collective-permute-start | bytes 786440 | tf_op jit(solution)/shard_map/ppermute | solution.py:13
  284.8 0.9 fusion.38
  285.7 0.9 fusion.37
  286.6 0.5 fusion.36
  287.1 0.4 copy-done.21
  287.5 0.7 add_add_fusion.1
  288.2 2.5 multiply_add_fusion
  290.7 1.0 fusion.14
  291.7 0.1 copy-done.7
  291.8 1.0 fusion.17
  292.8 2.1 multiply_convert_fusion
  294.9 15.9 %convert_bitcast_fusion = bf16[8192,1024]{0,1:T(8,128)(2,1)} fusion(bf16[512,8192]{1,0:T(8,128)(2,1)} %all-gather.3.cloned.1.call-done, f32[512,1024]{1,0:T(8,128)S(1)} %get-tuple-element.24, bf16[512,1024]{1,0:T(8,128)(2,1)S(1)} %copy-done.25), kind=kOutput, calls=%fused_computation | convolution fusion | flops 8599896064 | bytes 28311552 | tf_op jit(solution)/shard_map/dot_general | solution.py:75
  310.8 0.3 all-reduce.2.cloned.1.call-start
  311.0 1.0 copy-done.2
  312.0 0.4 copy-done.3
  312.4 0.5 fusion.25
  313.0 0.5 fusion.11
  313.6 0.4 copy-done.23
  313.9 1.4 fusion.12
  315.4 2.4 copy.26
  317.7 1.3 copy.25
  319.0 111.5 %reduce-scatter.2.cloned.1.call-done = bf16[1024,1024]{0,1:T(8,128)(2,1)} async-done(((bf16[8192,1024]{0,1:T(8,128)(2,1)}), bf16[1024,1024]{0,1:T(8,128)(2,1)}) %reduce-scatter.2.cloned.1.call-update) | async-done | bytes 2097168 | tf_op jit(solution)/shard_map/reduce_scatter | solution.py:78
  430.5 4.2 copy.27
  434.6 53.9 %all-reduce.2.cloned.1.call-done = f32[1024,128]{1,0:T(8,128)} async-done(((f32[1024,128]{1,0:T(8,128)}), f32[1024,128]{1,0:T(8,128)}) %all-reduce.2.cloned.1.call-update) | async-done | bytes 524304 | tf_op jit(solution)/shard_map/psum | solution.py:89
  488.6 1.9 copy.33
  (51 shorter events, 0.4 us)
Async XLA Ops:
  7.2 4.2 copy-start
  7.2 1.6 copy-start.10
  7.2 154.8 %all-gather.3.cloned.1.call-start = ((), (), s32[]{:S(2)}) async-start(), calls=%async_computation.1 | async-start | bytes 10485760 | tf_op jit(solution)/shard_map/all_gather | solution.py:64
  7.9 2.2 copy-start.11
  7.9 244.0 %all-gather.5.cloned.1.call-start = ((), (), s32[]{:S(2)}) async-start(), calls=%async_computation.2 | async-start | bytes 18874368 | tf_op jit(solution)/shard_map/all_gather | solution.py:65
  8.7 2.7 copy-start.20
  8.7 421.8 %reduce-scatter.2.cloned.1.call-start = ((), (), s32[]{:S(2)}) async-start(), calls=%async_computation.4 | async-start | bytes 18874368 | tf_op jit(solution)/shard_map/reduce_scatter | solution.py:78
  10.1 1.8 copy-start.13
  12.4 255.9 %copy-start.9 = (bf16[640,512]{1,0:T(8,128)(2,1)S(1)}, bf16[640,512]{1,0:T(8,128)(2,1)}, u32[]{:S(2)}) copy-start(bf16[640,512]{1,0:T(8,128)(2,1)} %constant.33) | copy-start | bytes 1966084
  266.9 2.3 copy-start.18
  266.9 3.6 collective-permute-start.1
  269.2 1.2 copy-start.22
  270.1 0.9 copy-start.24
  271.5 1.1 copy-start.8
  273.7 1.2 copy-start.5
  273.7 1.5 copy-start.6
  273.7 1.7 copy-start.12
  275.4 9.4 %copy-start.17 = (bf16[640,512]{1,0:T(8,128)(2,1)S(1)}, bf16[640,512]{1,0:T(8,128)(2,1)}, u32[]{:S(2)}) copy-start(bf16[640,512]{1,0:T(8,128)(2,1)} %constant.28) | copy-start | bytes 1966084
  278.1 7.6 %copy-start.16 = (bf16[640,512]{1,0:T(8,128)(2,1)S(1)}, bf16[640,512]{1,0:T(8,128)(2,1)}, u32[]{:S(2)}) copy-start(bf16[640,512]{1,0:T(8,128)(2,1)} %constant.25) | copy-start | bytes 1966084
  278.1 8.5 %collective-permute-start = (bf16[128,1024]{0,1:T(8,128)(2,1)S(1)}, bf16[128,1024]{0,1:T(8,128)(2,1)S(1)}, u32[]{:S(2)}, u32[]{:S(2)}) collective-permute-start(bf16[128,1024]{0,1:T(8,128)(2,1)S(1)} %slice.44), channel_id=1, source_target_pairs={{0,4},{4,8},{8,12},{12,16},{16,20},{20,24},{24,28},{1,5},{5,9},{9,... | collective-permute-start | bytes 786440 | tf_op jit(solution)/shard_map/ppermute | solution.py:13
  285.7 0.9 copy-start.14
  286.6 0.9 copy-start.21
  288.2 2.5 copy-start.15
  290.7 1.1 copy-start.7
  292.7 2.1 copy-start.25
  310.7 1.3 copy-start.2
  310.7 1.7 copy-start.3
  310.7 1.7 copy-start.19
  310.8 177.8 %all-reduce.2.cloned.1.call-start = ((), (), s32[]{:S(2)}) async-start(), calls=%async_computation.3 | async-start | bytes 1048576 | tf_op jit(solution)/shard_map/psum | solution.py:89
  313.0 0.9 copy-start.23
  315.3 2.4 copy-start.4
  430.5 60.0 %copy-start.1 = (bf16[1024,128]{1,0:T(8,128)(2,1)S(1)}, bf16[1024,128]{1,0:T(8,128)(2,1)}, u32[]{:S(2)}) copy-start(bf16[1024,128]{1,0:T(8,128)(2,1)} %param.17) | copy-start | bytes 786436
Sparse Core Ops, SparseCore 0:
  9.6 152.3 all-gather.2
  163.9 88.0 all-gather.4
  310.9 119.5 reduce-scatter.1
  434.0 54.5 all-reduce.1
where the time goes:
time: 498 us; the launch traced here: 497 us
  waiting for transfers between devices  407 us (82%)
  matrix products  48.7 us (10%)
  local copies, waits for them, and re-layouts  15.9 us (3%)
  between operations  14.1 us (3%)
  starting transfers between devices  8.5 us (2%)
    all_gather x1, waiting for transfers between devices, shards(): gathered = lax.all_gather(cotangent, 'ch', axis=1, tiled=True)  150 us
    reduce_scatter x1, waiting for transfers between devices, shards(): lax.psum_scatter(partial_grad, 'ctx', scatter_dimension=0, tiled=True)  111 us
    all_gather x1, waiting for transfers between devices, shards(): weight = lax.all_gather(proj_weight, 'ctx', axis=0, tiled=True)  90 us
    psum x1, waiting for transfers between devices, shards(): grad_filter = lax.psum(local_filter, 'ctx').T  53.9 us
    dot_general x20, matrix products, dot32(): return jnp.dot(a, b, preferred_element_type=jnp.float32)  32.9 us
    dot_general x1, matrix products, shards(): lax.dot_general(gathered, gated, (((0,), (0,)), ((), ())), preferred_elem...  15.9 us
    unnamed x58, local copies, waits for them, and re-layouts  15.9 us
  transfers between devices with their start and end apart: 6, of which 5 were waited for; matrix products, arithmetic and copies ran while one was open for 4% of the time, Pallas kernels for 0%

commit v1 on v0

--- a/solution.py
+++ b/solution.py
@@ -5,6 +5,18 @@
 from jax.sharding import PartitionSpec as P
 
 TAPS = 128
+
+
+def doubled_up(x, axis, dim):
+    ways, here = (lax.axis_size(axis), lax.axis_index(axis))
+    grown, reach = (x, 1)
+    while reach < ways:
+        theirs = lax.ppermute(grown, axis, [(d, d ^ reach) for d in range(ways)])
+        mine_first = jnp.concatenate([grown, theirs], axis=dim)
+        theirs_first = jnp.concatenate([theirs, grown], axis=dim)
+        grown = jnp.where(here & reach == 0, mine_first, theirs_first)
+        reach = 2 * reach
+    return grown
 
 
 def from_behind(x, axis, by):
@@ -62,7 +74,7 @@
     table = basis(points)
     inverse = (table.T / (points // 2)).astype(np.float32)
     gathered = lax.all_gather(cotangent, "ch", axis=1, tiled=True)
-    weight = lax.all_gather(proj_weight, "ctx", axis=0, tiled=True)
+    weight = doubled_up(proj_weight, "ctx", 0)
     query_f = query_act.astype(jnp.float32)
     key_f = key_act.astype(jnp.float32)
     value_f = value_act.astype(jnp.float32)

time: 498 us -> 555 us (1.11)
  waiting for transfers between devices: 407 us -> 437 us
  other arithmetic: 3.06 us -> 17.8 us
    ppermute x0 -> x3, waiting for transfers between devices: none -> 229 us  [doubled_up(): theirs = lax.ppermute(grown, axis, [(d, d ^ reach) for d in range(ways)])]
    all_gather x1, waiting for transfers between devices: 150 us -> 42.1 us  [shards(): gathered = lax.all_gather(cotangent, 'ch', axis=1, tiled=True)]
    all_gather x1 -> x0, waiting for transfers between devices: 90 us -> none  [shards(): weight = lax.all_gather(proj_weight, 'ctx', axis=0, tiled=True)]
    select_n x0 -> x2, other arithmetic: none -> 14.7 us  [doubled_up(): grown = jnp.where(here & reach == 0, mine_first, theirs_first)]
    unnamed x58 -> x62, local copies, waits for them, and re-layouts: 15.9 us -> 18.9 us
  transfers between devices with their start and end apart: 6 -> 8, of which waited for: 5 -> 7; matrix products, arithmetic and copies ran while one was open for 4% -> 5% of each run, Pallas kernels for 0% -> 0%
where the time goes in v1:
time: 555 us
  waiting for transfers between devices  437 us (79%)
  matrix products  53.2 us (10%)
  local copies, waits for them, and re-layouts  19.9 us (4%)
  other arithmetic  17.8 us (3%)
  between operations  14.1 us (3%)
  starting transfers between devices  13.1 us (2%)
    ppermute x3, waiting for transfers between devices, doubled_up(): theirs = lax.ppermute(grown, axis, [(d, d ^ reach) for d in range(ways)])  229 us
    reduce_scatter x1, waiting for transfers between devices, shards(): lax.psum_scatter(partial_grad, 'ctx', scatter_dimension=0, tiled=True)  111 us
    psum x1, waiting for transfers between devices, shards(): grad_filter = lax.psum(local_filter, 'ctx').T  54.1 us
    all_gather x1, waiting for transfers between devices, shards(): gathered = lax.all_gather(cotangent, 'ch', axis=1, tiled=True)  42.1 us
    dot_general x20, matrix products, dot32(): return jnp.dot(a, b, preferred_element_type=jnp.float32)  38.2 us
    unnamed x62, local copies, waits for them, and re-layouts  18.9 us
    dot_general x1, matrix products, shards(): lax.dot_general(gathered, gated, (((0,), (0,)), ((), ())), preferred_elem...  15.1 us
    select_n x2, other arithmetic, doubled_up(): grown = jnp.where(here & reach == 0, mine_first, theirs_first)  14.7 us
  transfers between devices with their start and end apart: 8, of which 7 were waited for; matrix products, arithmetic and copies ran while one was open for 5% of the time, Pallas kernels for 0%

profile of v1, /device:TPU:0, one launch (start us, length us, event | category | flops | bytes accessed | tf_op | source)
XLA Modules:
  0.0 554.8 jit_solution(6287772724912127776)
XLA Ops:
  7.2 0.5 collective-permute-start
  7.7 4.0 collective-permute-done
  11.7 4.7 maximum_select_fusion.3
  16.5 2.9 collective-permute-start.1
  19.4 91.1 %collective-permute-done.1 = bf16[2048,1024]{1,0:T(8,128)(2,1)} collective-permute-done((bf16[2048,1024]{1,0:T(8,128)(2,1)}, bf16[2048,1024]{1,0:T(8,128)(2,1)}, u32[]{:S(2)}, u32[]{:S(2)}) %collective-permute-start.1) | collective-permute-done | bytes 4194336 | tf_op jit(solution)/shard_map/ppermute | solution.py:14
  110.5 10.0 %maximum_select_fusion.2 = bf16[4096,1024]{1,0:T(8,128)(2,1)} fusion(bf16[2048,1024]{1,0:T(8,128)(2,1)} %collective-permute-done.1, bf16[2048,1024]{1,0:T(8,128)(2,1)} %maximum_select_fusion.3, pred[]{:T(512)S(6)} %eq.10), kind=kLoop, calls=%fused_computation.9 | loop fusion | flops 37748736 | bytes 16777216 | tf_op jit(solution)/shard_map/jit(_where)/select_n | solution.py:17
  120.5 1.8 collective-permute-start.2
  122.4 1.3 copy.22
  123.7 1.3 copy.19
  125.0 1.3 copy.20
  126.3 0.5 fusion.48
  126.9 0.5 convolution_add_fusion
  127.4 42.1 %all-gather.2.cloned.1.call-done = bf16[512,8192]{1,0:T(8,128)(2,1)} async-done(((bf16[512,2048]{1,0:T(8,128)(2,1)}), bf16[512,8192]{1,0:T(8,128)(2,1)}) %all-gather.2.cloned.1.call-update) | async-done | bytes 8388624 | tf_op jit(solution)/shard_map/all_gather | solution.py:76
  169.5 133.5 %collective-permute-done.2 = bf16[4096,1024]{1,0:T(8,128)(2,1)} collective-permute-done((bf16[4096,1024]{1,0:T(8,128)(2,1)}, bf16[4096,1024]{1,0:T(8,128)(2,1)}, u32[]{:S(2)}, u32[]{:S(2)}) %collective-permute-start.2) | collective-permute-done | bytes 8388640 | tf_op jit(solution)/shard_map/ppermute | solution.py:14
  302.9 18.6 %fusion.13 = (bf16[512,1024]{0,1:T(8,128)(2,1)}, f32[1024,512]{1,0:T(8,128)}) fusion(bf16[512,1024]{0,1:T(8,128)(2,1)} %copy.22, bf16[512,8192]{1,0:T(8,128)(2,1)} %all-gather.2.cloned.1.call-done, bf16[4096,1024]{1,0:T(8,128)(2,1)} %collective-permute-done.2, bf16[4096,1024]{1,0:T(8,128)(2,1)} %maximum_select_fusion.2, pred[]{:T(512)S(6)} %eq.9), kind=kOutput, calls=%fused_computation.30 | convolution fusion | flops 8667004928 | bytes 29360128 | tf_op jit(solution)/shard_map/dot_general | solution.py:42
  321.5 1.0 slice.49
  322.5 2.4 fusion.49
  324.9 1.6 collective-permute-start.4
  326.5 0.9 convolution_add_fusion.1
  327.4 1.0 collective-permute-done.4
  328.5 0.5 fusion.50
  329.0 0.5 add_add_fusion
  329.5 0.6 multiply_add_fusion.1
  330.6 1.0 fusion.29
  331.7 1.0 fusion.17
  333.4 2.8 fusion.10
  336.2 0.9 fusion.46
  337.1 6.2 %collective-permute-start.3 = (bf16[128,1024]{0,1:T(8,128)(2,1)S(1)}, bf16[128,1024]{0,1:T(8,128)(2,1)S(1)}, u32[]{:S(2)}, u32[]{:S(2)}) collective-permute-start(bf16[128,1024]{0,1:T(8,128)(2,1)S(1)} %slice.44), channel_id=1, source_target_pairs={{0,4},{4,8},{8,12},{12,16},{16,20},{20,24},{24,28},{1,5},{5,9},{9,... | collective-permute-start | bytes 786440 | tf_op jit(solution)/shard_map/ppermute | solution.py:25
  343.3 0.9 fusion.47
  344.2 0.5 fusion.45
  344.7 0.6 add_add_fusion.1
  345.3 2.5 multiply_add_fusion
  347.8 1.0 fusion.25
  348.9 1.0 fusion.16
  349.9 0.5 copy-done.11
  350.6 2.0 fusion.15
  352.6 15.1 %convert_bitcast_fusion = bf16[8192,1024]{0,1:T(8,128)(2,1)} fusion(bf16[512,8192]{1,0:T(8,128)(2,1)} %all-gather.2.cloned.1.call-done, f32[512,1024]{0,1:T(8,128)S(1)} %get-tuple-element.24, bf16[512,1024]{0,1:T(8,128)(2,1)S(1)} %copy-done.15), kind=kOutput, calls=%fused_computation.7 | convolution fusion | flops 8599896064 | bytes 28311552 | tf_op jit(solution)/shard_map/dot_general | solution.py:87
  367.8 1.2 copy-done.2
  369.4 0.5 fusion.33
  370.0 0.6 fusion.20
  370.9 1.4 fusion.21
  372.3 2.4 copy.26
  374.7 1.3 copy.27
  376.1 1.3 copy.25
  377.4 110.8 %reduce-scatter.2.cloned.1.call-done = bf16[1024,1024]{0,1:T(8,128)(2,1)} async-done(((bf16[8192,1024]{0,1:T(8,128)(2,1)}), bf16[1024,1024]{0,1:T(8,128)(2,1)}) %reduce-scatter.2.cloned.1.call-update) | async-done | bytes 2097168 | tf_op jit(solution)/shard_map/reduce_scatter | solution.py:90
  488.1 4.2 copy.28
  492.3 54.1 %all-reduce.2.cloned.1.call-done = f32[1024,128]{1,0:T(8,128)} async-done(((f32[1024,128]{1,0:T(8,128)}), f32[1024,128]{1,0:T(8,128)}) %all-reduce.2.cloned.1.call-update) | async-done | bytes 524304 | tf_op jit(solution)/shard_map/psum | solution.py:101
  546.4 1.9 copy.33
  (60 shorter events, 2.3 us)
Async XLA Ops:
  7.2 119.2 %copy-start = (bf16[1024,128]{1,0:T(8,128)(2,1)S(1)}, bf16[1024,128]{1,0:T(8,128)(2,1)}, u32[]{:S(2)}) copy-start(bf16[1024,128]{1,0:T(8,128)(2,1)} %param.17) | copy-start | bytes 786436
  7.2 162.3 %all-gather.2.cloned.1.call-start = ((), (), s32[]{:S(2)}) async-start(), calls=%async_computation.1 | async-start | bytes 10485760 | tf_op jit(solution)/shard_map/all_gather | solution.py:76
  7.2 4.5 collective-permute-start
  16.5 94.0 %collective-permute-start.1 = (bf16[2048,1024]{1,0:T(8,128)(2,1)}, bf16[2048,1024]{1,0:T(8,128)(2,1)}, u32[]{:S(2)}, u32[]{:S(2)}) collective-permute-start(bf16[2048,1024]{1,0:T(8,128)(2,1)} %maximum_select_fusion.3), channel_id=1, source_target_pairs={{0,8},{4,12},{8,0},{12,4},{16,24},{20,28},{24,16},{28,20},{1,9},{5... | collective-permute-start | bytes 12582920 | tf_op jit(solution)/shard_map/ppermute | solution.py:14
  19.3 468.8 %reduce-scatter.2.cloned.1.call-start = ((), (), s32[]{:S(2)}) async-start(), calls=%async_computation.3 | async-start | bytes 18874368 | tf_op jit(solution)/shard_map/reduce_scatter | solution.py:90
  19.4 103.0 %copy-start.12 = (bf16[512,1024]{1,0:T(8,128)(2,1)S(1)}, bf16[512,1024]{1,0:T(8,128)(2,1)}, u32[]{:S(2)}) copy-start(bf16[512,1024]{1,0:T(8,128)(2,1)} %param.14) | copy-start | bytes 3145732
  120.5 3.2 copy-start.13
  120.5 4.5 copy-start.14
  120.5 182.4 %collective-permute-start.2 = (bf16[4096,1024]{1,0:T(8,128)(2,1)}, bf16[4096,1024]{1,0:T(8,128)(2,1)}, u32[]{:S(2)}, u32[]{:S(2)}) collective-permute-start(bf16[4096,1024]{1,0:T(8,128)(2,1)} %maximum_select_fusion.2), channel_id=1, source_target_pairs={{0,16},{4,20},{8,24},{12,28},{16,0},{20,4},{24,8},{28,12},{1,17},{... | collective-permute-start | bytes 25165832 | tf_op jit(solution)/shard_map/ppermute | solution.py:14
  123.7 2.6 copy-start.23
  125.0 1.8 copy-start.18
  322.4 4.1 copy-start.4
  322.4 4.1 copy-start.21
  324.9 3.6 copy-start.24
  324.9 3.6 collective-permute-start.4
  327.4 1.6 copy-start.26
  329.5 1.1 copy-start.10
  331.6 1.2 copy-start.6
  331.7 1.5 copy-start.7
  331.7 1.7 copy-start.17
  333.4 2.8 copy-start.20
  336.2 7.1 %copy-start.19 = (bf16[640,512]{1,0:T(8,128)(2,1)S(1)}, bf16[640,512]{1,0:T(8,128)(2,1)}, u32[]{:S(2)}) copy-start(bf16[640,512]{1,0:T(8,128)(2,1)} %constant.42) | copy-start | bytes 1966084
  337.1 7.1 %collective-permute-start.3 = (bf16[128,1024]{0,1:T(8,128)(2,1)S(1)}, bf16[128,1024]{0,1:T(8,128)(2,1)S(1)}, u32[]{:S(2)}, u32[]{:S(2)}) collective-permute-start(bf16[128,1024]{0,1:T(8,128)(2,1)S(1)} %slice.44), channel_id=1, source_target_pairs={{0,4},{4,8},{8,12},{12,16},{16,20},{20,24},{24,28},{1,5},{5,9},{9,... | collective-permute-start | bytes 786440 | tf_op jit(solution)/shard_map/ppermute | solution.py:25
  345.3 2.5 copy-start.9
  348.9 1.6 copy-start.11
  348.9 1.7 copy-start.16
  350.6 2.0 copy-start.15
  367.7 1.3 copy-start.2
  367.7 1.7 copy-start.3
  367.7 1.7 copy-start.22
  367.7 178.6 %all-reduce.2.cloned.1.call-start = ((), (), s32[]{:S(2)}) async-start(), calls=%async_computation.2 | async-start | bytes 1048576 | tf_op jit(solution)/shard_map/psum | solution.py:101
  370.0 0.9 copy-start.25
  372.3 2.5 copy-start.5
  372.3 3.7 copy-start.8
  488.1 60.1 %copy-start.1 = (bf16[1024,128]{1,0:T(8,128)(2,1)S(1)}, bf16[1024,128]{1,0:T(8,128)(2,1)}, u32[]{:S(2)}) copy-start(bf16[1024,128]{1,0:T(8,128)(2,1)} %param.17) | copy-start | bytes 786436
Sparse Core Ops, SparseCore 0:
  19.5 149.9 all-gather.1
  367.8 120.2 reduce-scatter.1
  491.8 54.5 all-reduce.1
